TPU v7x, 32 devices: a whole 2x2x4 slice. The times are simulated.
32 devices in a mesh: gx: 2 (over x), gy: 4 (over y, core), gz: 4 (over z).
Axes of the slice: x: 2, y: 2, z: 4, core: 2. Of those that a mesh axis runs over, the one named last changes fastest.
Arguments:
- solution_in: float32 [16, 128, 512], P('gx', 'gy', 'gz'), may hold values from -6 to 6
- residual_in: float32 [16, 128, 512], P('gx', 'gy', 'gz'), may hold values from -12 to 12
- direction_in: float32 [16, 128, 512], P('gx', 'gy', 'gz'), may hold values from -6 to 6
- material: int32 [16, 128, 512], P('gx', 'gy', 'gz'), may hold values from 0 to 7
- cond_table: float32 [8], replicated, may hold values from 0.5 to 4
- cap_table: float32 [8], replicated, may hold values from 0.2 to 1
- gas_flux: float32 [128, 512], P('gy', 'gz'), may hold values from -6 to 6
- supply_map: int32 [128, 512], P('gy', 'gz'), may hold values from 0 to 511, as said below
Outputs:
- solution: float32 [16, 128, 512], P('gx', 'gy', 'gz')
- residual: float32 [16, 128, 512], P('gx', 'gy', 'gz')
- direction: float32 [16, 128, 512], P('gx', 'gy', 'gz')
Inputs may be any that keep to these rules, and one draw needn't show every extreme that they name: `supply_map`: the gas faces are laid out so that the faces held by index q of gz, in their slots t * 128 / 4 to (t + 1) * 128 / 4 - 1, supply solid faces held by index t of gz in the same row; every gas face supplies exactly one solid face of its row.
All inputs are finite; a program needn't handle non-finite values.
Results may differ from a plain program's by a relative error of at most 0.0006.
Values sent between devices are 32-bit elements; how exact they have to be, the bound alone decides.
A program may use at most 64 MiB of HBM per device.

v0:
```python
import jax
import jax.numpy as jnp
from jax import lax
from jax.sharding import PartitionSpec as P

STEPS = 4


def extended(block, sides, width):
    for axis, dim in sides:
        count = lax.axis_size(axis)
        forward = [(i, i + 1) for i in range(count - 1)]
        backward = [(target, source) for source, target in forward]
        low = lax.ppermute(
            lax.slice_in_dim(block, block.shape[dim] - width, None, axis=dim), axis, forward
        )
        high = lax.ppermute(lax.slice_in_dim(block, 0, width, axis=dim), axis, backward)
        block = jnp.concatenate([low, block, high], axis=dim)
    return block


def harmonic(lower_side, upper_side):
    return (
        2.0
        * lower_side
        * upper_side
        / (jnp.where(lower_side > 0, lower_side, 1.0) + jnp.where(upper_side > 0, upper_side, 1.0))
    )


def face_terms(cond):
    return (
        harmonic(cond[:-1], cond[1:]),
        harmonic(cond[:, :-1], cond[:, 1:]),
        harmonic(cond[:, :, :-1], cond[:, :, 1:]),
    )


def operate(values, capacity, conductance):
    result = capacity * values
    face_flow = conductance[0] * (values[1:] - values[:-1])
    result = (
        result
        - jnp.pad(face_flow, ((0, 1), (0, 0), (0, 0)))
        + jnp.pad(face_flow, ((1, 0), (0, 0), (0, 0)))
    )
    face_flow = conductance[1] * (values[:, 1:] - values[:, :-1])
    result = (
        result
        - jnp.pad(face_flow, ((0, 0), (0, 1), (0, 0)))
        + jnp.pad(face_flow, ((0, 0), (1, 0), (0, 0)))
    )
    face_flow = conductance[2] * (values[:, :, 1:] - values[:, :, :-1])
    result = (
        result
        - jnp.pad(face_flow, ((0, 0), (0, 0), (0, 1)))
        + jnp.pad(face_flow, ((0, 0), (0, 0), (1, 0)))
    )
    return result


def lookup_code(codes, table):
    summed = jnp.zeros(codes.shape, jnp.float32)
    for material_id in range(table.shape[0]):
        summed = summed + jnp.where(
            codes == jnp.float32(material_id + 1), table[material_id], jnp.float32(0.0)
        )
    return summed


def spectrum(cond_table, cap_table):
    lowest = jnp.min(cap_table)
    highest = jnp.max(cap_table) + 12.0 * jnp.max(cond_table)
    return (0.5 * (highest + lowest), 0.5 * (highest - lowest))


def next_term(applied, terms, center, half_width):
    shifted = (applied - center * terms[-1]) / half_width
    if len(terms) == 1:
        return shifted
    return 2.0 * shifted - terms[-2]


def shift_matrix(center, half_width, steps):
    dimension = 2 * steps + 1
    matrix = jnp.zeros((dimension, dimension), jnp.float32)
    for offset, length in ((0, steps + 1), (steps + 1, steps)):
        for column in range(length - 1):
            matrix = matrix.at[offset + column, offset + column].set(center)
            matrix = matrix.at[offset + column + 1, offset + column].set(
                half_width if column == 0 else 0.5 * half_width
            )
            if column >= 1:
                matrix = matrix.at[offset + column - 1, offset + column].set(0.5 * half_width)
    return matrix


def coefficients(gram, center, half_width, steps):
    dimension = 2 * steps + 1
    matrix = shift_matrix(center, half_width, steps)
    highest_prec = lax.Precision.HIGHEST

    def gram_product(first_vec, second_vec):
        return jnp.dot(
            first_vec, jnp.dot(gram, second_vec, precision=highest_prec), precision=highest_prec
        )

    direct = jnp.zeros((dimension,), jnp.float32).at[0].set(1.0)
    residue = jnp.zeros((dimension,), jnp.float32).at[steps + 1].set(1.0)
    moved = jnp.zeros((dimension,), jnp.float32)
    norm_now = gram_product(residue, residue)
    for sweep in range(steps):
        mapped = jnp.dot(matrix, direct, precision=highest_prec)
        step_length = norm_now / gram_product(direct, mapped)
        moved = moved + step_length * direct
        residue = residue - step_length * mapped
        norm_next = gram_product(residue, residue)
        direct = residue + norm_next / norm_now * direct
        norm_now = norm_next
    return (moved, residue, direct)


def combine(weights, basis):
    summed = weights[0] * basis[0]
    for position in range(1, len(basis)):
        summed = summed + weights[position] * basis[position]
    return summed


def inside(values, depth):
    return values[depth:-depth, depth:-depth, depth:-depth]


def body(
    solution_in, residual_in, direction_in, material, cond_table, cap_table, gas_flux, supply_map
):
    surface_rows, surface_width = gas_flux.shape
    groups = lax.axis_size("gz")
    segment = surface_width // groups
    arrived = lax.all_to_all(
        gas_flux.reshape(surface_rows, groups, segment),
        "gz",
        split_axis=1,
        concat_axis=1,
        tiled=True,
    )
    arrived = arrived.reshape(surface_rows, surface_width)
    slot = (
        supply_map // surface_width * segment
        + supply_map % surface_width
        - lax.axis_index("gz") * segment
    )
    incoming = jnp.take_along_axis(arrived, slot, axis=1)
    is_top = lax.axis_index("gx") == lax.axis_size("gx") - 1
    start = residual_in.at[-1].add(jnp.where(is_top, incoming, jnp.float32(0.0)))
    codes = (material + 1).astype(jnp.float32)
    center, half_width = spectrum(cond_table, cap_table)
    first = extended(jnp.stack([direction_in, start, codes]), (("gx", 1), ("gy", 2), ("gz", 3)), 1)
    conductance = face_terms(lookup_code(first[2], cond_table))
    capacity_ext = lookup_code(first[2], cap_table)
    dir_terms = [direction_in]
    res_terms = [start]
    dir_applied = inside(operate(first[0], capacity_ext, conductance), 1)
    res_applied = inside(operate(first[1], capacity_ext, conductance), 1)
    res_terms.append(next_term(res_applied, res_terms, center, half_width))
    dir_terms.append(next_term(dir_applied, dir_terms, center, half_width))
    for sweep in range(1, STEPS):
        if sweep < STEPS - 1:
            layered = extended(
                jnp.stack([dir_terms[-1], res_terms[-1]]), (("gx", 1), ("gy", 2), ("gz", 3)), 1
            )
            dir_applied = inside(operate(layered[0], capacity_ext, conductance), 1)
            res_applied = inside(operate(layered[1], capacity_ext, conductance), 1)
            res_terms.append(next_term(res_applied, res_terms, center, half_width))
        else:
            layered = extended(dir_terms[-1], (("gx", 0), ("gy", 1), ("gz", 2)), 1)
            dir_applied = inside(operate(layered, capacity_ext, conductance), 1)
        dir_terms.append(next_term(dir_applied, dir_terms, center, half_width))
    basis = dir_terms + res_terms
    stacked = jnp.stack([term.reshape(-1) for term in basis])
    partial_gram = jnp.dot(stacked, stacked.T, precision=lax.Precision.HIGHEST)
    gram = lax.psum(partial_gram, ("gx", "gy", "gz"))
    moved, residue, direct = coefficients(gram, center, half_width, STEPS)
    return (solution_in + combine(moved, basis), combine(residue, basis), combine(direct, basis))


def solution(mesh):
    in_specs = (
        P("gx", "gy", "gz"),
        P("gx", "gy", "gz"),
        P("gx", "gy", "gz"),
        P("gx", "gy", "gz"),
        P(),
        P(),
        P("gy", "gz"),
        P("gy", "gz"),
    )
    out_specs = (P("gx", "gy", "gz"), P("gx", "gy", "gz"), P("gx", "gy", "gz"))
    return jax.shard_map(body, mesh=mesh, in_specs=in_specs, out_specs=out_specs, check_vma=False)
```

profile of v0, /device:TPU:0, one launch (start us, length us, event | category | flops | bytes accessed | tf_op | source)
XLA Modules:
  0.0 260.0 jit_solution(15775123754584945129)
XLA Ops:
  2.2 6.3 %all-to-all-start = ((f32[4,1,1024]{2,1,0:T(1,128)}), f32[4,1,1024]{2,1,0:T(1,128)S(1)}, u32[]{:S(2)}, u32[]{:S(2)}) async-start(f32[4,1,1024]{2,1,0:T(1,128)} %reshape.745), calls=%async_computation | async-start | bytes 32768 | tf_op jit(solution)/shard_map/all_to_all | solution.py:140
  10.2 3.9 %all-to-all-done = f32[4,1,1024]{2,1,0:T(1,128)S(1)} async-done(((f32[4,1,1024]{2,1,0:T(1,128)}), f32[4,1,1024]{2,1,0:T(1,128)S(1)}, u32[]{:S(2)}, u32[]{:S(2)}) %all-to-all-start) | async-done | bytes 16416 | tf_op jit(solution)/shard_map/all_to_all | solution.py:140
  15.6 25.6 %gather_fusion = f32[4096]{0:T(1024)S(1)} fusion(f32[32,128]{1,0:T(8,128)S(1)} %reshape.660, s32[4096]{0:T(1024)S(1)} %fusion.80), kind=kCustom, calls=%fused_computation | custom fusion | bytes 65536 | tf_op jit(solution)/shard_map/jit(take_along_axis)/gather | solution.py:153
  41.3 3.4 %collective-permute-start = (f32[3,1,32,128]{3,2,1,0:T(8,128)S(1)}, f32[3,1,32,128]{3,2,1,0:T(8,128)S(1)}, u32[]{:S(2)}, u32[]{:S(2)}) collective-permute-start(f32[3,1,32,128]{3,2,1,0:T(8,128)S(1)} %get-tuple-element.320), channel_id=1, source_target_pairs={{0,16},{1,17},{2,18},{3,19},{4,20},{5,21},{6,22},{7,23},{8,24},{9,... | collective-permute-start | bytes 147464 | tf_op jit(solution)/shard_map/ppermute | solution.py:14
  44.7 1.3 collective-permute-start.1
  46.7 4.0 %collective-permute-done.1 = f32[3,1,32,128]{3,2,1,0:T(8,128)S(1)} collective-permute-done((f32[3,1,32,128]{3,2,1,0:T(8,128)S(1)}, f32[3,1,32,128]{3,2,1,0:T(8,128)S(1)}, u32[]{:S(2)}, u32[]{:S(2)}) %collective-permute-start.1) | collective-permute-done | bytes 49184 | tf_op jit(solution)/shard_map/ppermute | solution.py:17
  52.0 1.3 collective-permute-start.3
  54.0 2.8 %collective-permute-done.3 = f32[3,10,1,128]{3,2,1,0:T(1,128)S(1)} collective-permute-done((f32[3,10,1,128]{3,2,1,0:T(1,128)S(1)}, f32[3,10,1,128]{3,2,1,0:T(1,128)S(1)}, u32[]{:S(2)}, u32[]{:S(2)}) %collective-permute-start.3) | collective-permute-done | bytes 15392 | tf_op jit(solution)/shard_map/ppermute | solution.py:17
  57.4 2.6 collective-permute-start.4
  67.0 5.8 %bitcast_multiply_fusion.6 = (f32[10,34,130]{2,1,0:T(8,128)S(1)}, f32[1,10,34,130]{3,2,1,0:T(8,128)S(1)}, pred[1,10,34,130]{3,2,1,0:T(8,128)(4,1)S(1)}, pred[1,1...) fusion(f32[3,10,34,130]{3,2,1,0:T(8,128)S(1)} %pad_maximum_fusi, ...), kind=kLoop, calls=%fused_computation.85 | loop fusion | flops 1060800 | bytes 1060832 | tf_op jit(solution)/shard_map/mul | solution.py:40
  72.8 5.4 %add_add_fusion = f32[1,10,34,130]{3,2,1,0:T(8,128)S(1)} fusion(pred[1,10,34,130]{3,2,1,0:T(8,128)(4,1)S(1)} %get-tuple-element.283, pred[1,10,34,130]{3,2,1,0:T(8,128)(4,1)S(1)} %get-tuple-element.282, pred[1,10,34,130]{3,2,1,0:T(8,128)(4,1)S(1)} %get-tuple-element.281, pred[1,10,34,130]{3,2,1,0:T(8,128)(4,1)S(1)} %get-tuple-element.280, ...), kind=kLoop, calls=%fused_computation.86 | loop fusion | flops 663000 | bytes 530432 | tf_op jit(solution)/shard_map/add | solution.py:65
  79.7 1.6 collective-permute-start.6
  81.3 1.3 collective-permute-start.7
  82.8 4.2 %collective-permute-done.7 = f32[2,1,32,128]{3,2,1,0:T(8,128)S(1)} collective-permute-done((f32[2,1,32,128]{3,2,1,0:T(8,128)S(1)}, f32[2,1,32,128]{3,2,1,0:T(8,128)S(1)}, u32[]{:S(2)}, u32[]{:S(2)}) %collective-permute-start.7) | collective-permute-done | bytes 32800 | tf_op jit(solution)/shard_map/ppermute | solution.py:17
  87.1 2.4 collective-permute-start.8
  89.5 1.3 collective-permute-start.9
  90.8 3.3 %collective-permute-done.9 = f32[2,10,1,128]{3,2,1,0:T(1,128)S(1)} collective-permute-done((f32[2,10,1,128]{3,2,1,0:T(1,128)S(1)}, f32[2,10,1,128]{3,2,1,0:T(1,128)S(1)}, u32[]{:S(2)}, u32[]{:S(2)}) %collective-permute-start.9) | collective-permute-done | bytes 10272 | tf_op jit(solution)/shard_map/ppermute | solution.py:17
  94.3 4.3 %collective-permute-start.10 = (f32[2,10,34,1]{3,2,1,0:T(8,128)S(1)}, f32[2,10,34,1]{3,2,1,0:T(8,128)S(1)}, u32[]{:S(2)}, u32[]{:S(2)}) collective-permute-start(f32[2,10,34,1]{3,2,1,0:T(8,128)S(1)} %get-tuple-element.318), channel_id=1, source_target_pairs={{0,1},{1,2},{2,3},{4,5},{5,6},{6,7},{8,9},{9,10},{10,11},{12,13},{... | collective-permute-start | bytes 8168 | tf_op jit(solution)/shard_map/ppermute | solution.py:14
  98.6 1.3 collective-permute-start.11
  99.9 7.0 %collective-permute-done.10 = f32[2,10,34,1]{3,2,1,0:T(8,128)S(1)} collective-permute-done((f32[2,10,34,1]{3,2,1,0:T(8,128)S(1)}, f32[2,10,34,1]{3,2,1,0:T(8,128)S(1)}, u32[]{:S(2)}, u32[]{:S(2)}) %collective-permute-start.10) | collective-permute-done | bytes 2752 | tf_op jit(solution)/shard_map/ppermute | solution.py:14
  106.9 4.7 %collective-permute-done.11 = f32[2,10,34,1]{3,2,1,0:T(8,128)S(1)} collective-permute-done((f32[2,10,34,1]{3,2,1,0:T(8,128)S(1)}, f32[2,10,34,1]{3,2,1,0:T(8,128)S(1)}, u32[]{:S(2)}, u32[]{:S(2)}) %collective-permute-start.11) | collective-permute-done | bytes 2752 | tf_op jit(solution)/shard_map/ppermute | solution.py:17
  113.4 1.6 collective-permute-start.12
  115.0 1.3 collective-permute-start.13
  116.7 4.2 %collective-permute-done.13 = f32[2,1,32,128]{3,2,1,0:T(8,128)S(1)} collective-permute-done((f32[2,1,32,128]{3,2,1,0:T(8,128)S(1)}, f32[2,1,32,128]{3,2,1,0:T(8,128)S(1)}, u32[]{:S(2)}, u32[]{:S(2)}) %collective-permute-start.13) | collective-permute-done | bytes 32800 | tf_op jit(solution)/shard_map/ppermute | solution.py:17
  120.9 1.8 collective-permute-start.14
  122.7 1.3 collective-permute-start.15
  124.0 1.9 collective-permute-done.15
  126.2 2.4 collective-permute-start.16
  128.6 1.3 collective-permute-start.17
  129.9 7.0 %collective-permute-done.16 = f32[2,10,34,1]{3,2,1,0:T(8,128)S(1)} collective-permute-done((f32[2,10,34,1]{3,2,1,0:T(8,128)S(1)}, f32[2,10,34,1]{3,2,1,0:T(8,128)S(1)}, u32[]{:S(2)}, u32[]{:S(2)}) %collective-permute-start.16) | collective-permute-done | bytes 2752 | tf_op jit(solution)/shard_map/ppermute | solution.py:14
  136.9 4.7 %collective-permute-done.17 = f32[2,10,34,1]{3,2,1,0:T(8,128)S(1)} collective-permute-done((f32[2,10,34,1]{3,2,1,0:T(8,128)S(1)}, f32[2,10,34,1]{3,2,1,0:T(8,128)S(1)}, u32[]{:S(2)}, u32[]{:S(2)}) %collective-permute-start.17) | collective-permute-done | bytes 2752 | tf_op jit(solution)/shard_map/ppermute | solution.py:17
  144.4 1.6 collective-permute-start.18
  146.1 1.3 collective-permute-start.19
  147.5 4.2 %collective-permute-done.19 = f32[1,32,128]{2,1,0:T(8,128)S(1)} collective-permute-done((f32[1,32,128]{2,1,0:T(8,128)S(1)}, f32[1,32,128]{2,1,0:T(8,128)S(1)}, u32[]{:S(2)}, u32[]{:S(2)}) %collective-permute-start.19) | collective-permute-done | bytes 16416 | tf_op jit(solution)/shard_map/ppermute | solution.py:17
  151.7 1.5 collective-permute-start.20
  153.2 1.3 collective-permute-start.21
  156.1 1.9 dynamic-slice.147
  159.2 1.4 scatter.70
  163.1 2.5 collective-permute-start.22
  165.6 1.3 collective-permute-start.23
  167.0 3.3 %collective-permute-done.22 = f32[10,34,1]{2,1,0:T(8,128)S(1)} collective-permute-done((f32[10,34,1]{2,1,0:T(8,128)S(1)}, f32[10,34,1]{2,1,0:T(8,128)S(1)}, u32[]{:S(2)}, u32[]{:S(2)}) %collective-permute-start.22) | collective-permute-done | bytes 1392 | tf_op jit(solution)/shard_map/ppermute | solution.py:14
  170.3 4.7 %collective-permute-done.23 = f32[10,34,1]{2,1,0:T(8,128)S(1)} collective-permute-done((f32[10,34,1]{2,1,0:T(8,128)S(1)}, f32[10,34,1]{2,1,0:T(8,128)S(1)}, u32[]{:S(2)}, u32[]{:S(2)}) %collective-permute-start.23) | collective-permute-done | bytes 1392 | tf_op jit(solution)/shard_map/ppermute | solution.py:17
  178.1 1.9 stack.43
  180.0 2.9 %fusion.119 = f32[9,9]{1,0:T(8,128)S(1)} fusion(f32[9,32768]{1,0:T(8,128)S(1)} %stack.43), kind=kOutput, calls=%fused_computation.275 | convolution fusion | flops 31850496 | bytes 1179972 | tf_op jit(solution)/shard_map/dot_general | solution.py:181
  183.0 38.1 %psum.7 = f32[9,9]{1,0:T(8,128)S(1)} all-reduce(f32[9,9]{1,0:T(8,128)S(1)} %fusion.119), channel_id=1, replica_groups=mesh['gx'=2,'gy'=4,'gz'=4] {'gx','gy','gz'}, use_global_device_ids=true, to_apply=%region_3.4 | all-reduce | flops 81 | bytes 648 | tf_op jit(solution)/shard_map/psum | solution.py:182
  240.9 6.2 %multiply_add_fusion = f32[8,32,128]{2,1,0:T(8,128)} fusion(f32[8,32,128]{2,1,0:T(8,128)S(1)} %fusion.54, f32[8,32,128]{2,1,0:T(8,128)S(1)} %fusion.66, f32[8,32,128]{2,1,0:T(8,128)S(1)} %get-tuple-element.383, f32[8,32,128]{2,1,0:T(8,128)S(1)} %fusion.78, f32[8,32,128]{2,1,0:T(8,128)S(1)} %fusion.58, f32[8,32,128]{2,1,0:T(8,128)S(1)} %fusion.62, ...), kind=kLoop, calls=%fused_computation.187 | loop fusion | flops 557056 | bytes 1310756 | tf_op jit(solution)/shard_map/add | solution.py:126
  247.2 6.4 %multiply_add_fusion.1 = f32[8,32,128]{2,1,0:T(8,128)} fusion(f32[8,32,128]{2,1,0:T(8,128)S(1)} %fusion.54, f32[8,32,128]{2,1,0:T(8,128)S(1)} %fusion.66, f32[8,32,128]{2,1,0:T(8,128)S(1)} %get-tuple-element.383, f32[8,32,128]{2,1,0:T(8,128)S(1)} %fusion.78, f32[8,32,128]{2,1,0:T(8,128)S(1)} %fusion.58, f32[8,32,128]{2,1,0:T(8,128)S(1)} %fusion.62, ...), kind=kLoop, calls=%fused_computation.188 | loop fusion | flops 557056 | bytes 1310756 | tf_op jit(solution)/shard_map/add | solution.py:126
  253.6 6.4 %add_add_fusion.2 = f32[8,32,128]{2,1,0:T(8,128)} fusion(f32[8,32,128]{2,1,0:T(8,128)S(1)} %copy-done.3, f32[8,32,128]{2,1,0:T(8,128)S(1)} %fusion.54, f32[8,32,128]{2,1,0:T(8,128)S(1)} %fusion.66, f32[8,32,128]{2,1,0:T(8,128)S(1)} %get-tuple-element.383, f32[8,32,128]{2,1,0:T(8,128)S(1)} %fusion.78, f32[8,32,128]{2,1,0:T(8,128)S(1)} %fusion.58, ...), kind=kLoop, calls=%fused_computation.189 | loop fusion | flops 589824 | bytes 1441828 | tf_op jit(solution)/shard_map/add | solution.py:184
  (145 shorter events, 35.9 us)
Async XLA Ops:
  2.2 11.9 %all-to-all-start = ((f32[4,1,1024]{2,1,0:T(1,128)}), f32[4,1,1024]{2,1,0:T(1,128)S(1)}, u32[]{:S(2)}, u32[]{:S(2)}) async-start(f32[4,1,1024]{2,1,0:T(1,128)} %reshape.745), calls=%async_computation | async-start | bytes 32768 | tf_op jit(solution)/shard_map/all_to_all | solution.py:140
  15.5 25.7 %copy-start = (f32[8,32,128]{2,1,0:T(8,128)S(1)}, f32[8,32,128]{2,1,0:T(8,128)}, u32[]{:S(2)}) copy-start(f32[8,32,128]{2,1,0:T(8,128)} %param.53) | copy-start | bytes 393220
  15.5 25.7 %copy-start.4 = (s32[32,128]{1,0:T(8,128)S(1)}, s32[32,128]{1,0:T(8,128)}, u32[]{:S(2)}) copy-start(s32[32,128]{1,0:T(8,128)} %param.59) | copy-start | bytes 49156
  15.6 25.7 %copy-start.1 = (f32[8,32,128]{2,1,0:T(8,128)S(1)}, f32[8,32,128]{2,1,0:T(8,128)}, u32[]{:S(2)}) copy-start(f32[8,32,128]{2,1,0:T(8,128)} %param.54) | copy-start | bytes 393220
  15.6 30.4 %copy-start.5 = (f32[8]{0:T(128)S(1)}, f32[8]{0:T(128)}, u32[]{:S(2)}) copy-start(f32[8]{0:T(128)} %param.57) | copy-start | bytes 100
  15.6 37.7 %copy-start.6 = (f32[8]{0:T(128)S(1)}, f32[8]{0:T(128)}, u32[]{:S(2)}) copy-start(f32[8]{0:T(128)} %param.56) | copy-start | bytes 100
  41.3 5.4 %collective-permute-start = (f32[3,1,32,128]{3,2,1,0:T(8,128)S(1)}, f32[3,1,32,128]{3,2,1,0:T(8,128)S(1)}, u32[]{:S(2)}, u32[]{:S(2)}) collective-permute-start(f32[3,1,32,128]{3,2,1,0:T(8,128)S(1)} %get-tuple-element.320), channel_id=1, source_target_pairs={{0,16},{1,17},{2,18},{3,19},{4,20},{5,21},{6,22},{7,23},{8,24},{9,... | collective-permute-start | bytes 147464 | tf_op jit(solution)/shard_map/ppermute | solution.py:14
  44.7 6.0 %collective-permute-start.1 = (f32[3,1,32,128]{3,2,1,0:T(8,128)S(1)}, f32[3,1,32,128]{3,2,1,0:T(8,128)S(1)}, u32[]{:S(2)}, u32[]{:S(2)}) collective-permute-start(f32[3,1,32,128]{3,2,1,0:T(8,128)S(1)} %get-tuple-element.321), channel_id=1, source_target_pairs={{16,0},{17,1},{18,2},{19,3},{20,4},{21,5},{22,6},{23,7},{24,8},{25... | collective-permute-start | bytes 147464 | tf_op jit(solution)/shard_map/ppermute | solution.py:17
  50.7 3.3 %collective-permute-start.2 = (f32[3,10,1,128]{3,2,1,0:T(1,128)S(1)}, f32[3,10,1,128]{3,2,1,0:T(1,128)S(1)}, u32[]{:S(2)}, u32[]{:S(2)}) collective-permute-start(f32[3,10,1,128]{3,2,1,0:T(1,128)S(1)} %get-tuple-element.306), channel_id=1, source_target_pairs={{0,4},{4,8},{8,12},{1,5},{5,9},{9,13},{2,6},{6,10},{10,14},{3,7},{... | collective-permute-start | bytes 46088 | tf_op jit(solution)/shard_map/ppermute | solution.py:14
  52.0 4.8 %collective-permute-start.3 = (f32[3,10,1,128]{3,2,1,0:T(1,128)S(1)}, f32[3,10,1,128]{3,2,1,0:T(1,128)S(1)}, u32[]{:S(2)}, u32[]{:S(2)}) collective-permute-start(f32[3,10,1,128]{3,2,1,0:T(1,128)S(1)} %get-tuple-element.307), channel_id=1, source_target_pairs={{4,0},{8,4},{12,8},{5,1},{9,5},{13,9},{6,2},{10,6},{14,10},{7,3},{... | collective-permute-start | bytes 46088 | tf_op jit(solution)/shard_map/ppermute | solution.py:17
  57.4 7.8 %collective-permute-start.4 = (f32[3,10,34,1]{2,3,1,0:T(1,128)S(1)}, f32[3,10,34,1]{2,3,1,0:T(1,128)S(1)}, u32[]{:S(2)}, u32[]{:S(2)}) collective-permute-start(f32[3,10,34,1]{2,3,1,0:T(1,128)S(1)} %copy.31), channel_id=1, source_target_pairs={{0,1},{1,2},{2,3},{4,5},{5,6},{6,7},{8,9},{9,10},{10,11},{12,13},{... | collective-permute-start | bytes 12248 | tf_op jit(solution)/shard_map/ppermute | solution.py:14
  60.3 5.6 %collective-permute-start.5 = (f32[3,10,34,1]{2,3,1,0:T(1,128)S(1)}, f32[3,10,34,1]{2,3,1,0:T(1,128)S(1)}, u32[]{:S(2)}, u32[]{:S(2)}) collective-permute-start(f32[3,10,34,1]{2,3,1,0:T(1,128)S(1)} %copy.32), channel_id=1, source_target_pairs={{1,0},{2,1},{3,2},{5,4},{6,5},{7,6},{9,8},{10,9},{11,10},{13,12},{... | collective-permute-start | bytes 12248 | tf_op jit(solution)/shard_map/ppermute | solution.py:17
  79.7 3.2 %collective-permute-start.6 = (f32[2,1,32,128]{3,2,1,0:T(8,128)S(1)}, f32[2,1,32,128]{3,2,1,0:T(8,128)S(1)}, u32[]{:S(2)}, u32[]{:S(2)}) collective-permute-start(f32[2,1,32,128]{3,2,1,0:T(8,128)S(1)} %get-tuple-element.328), channel_id=1, source_target_pairs={{0,16},{1,17},{2,18},{3,19},{4,20},{5,21},{6,22},{7,23},{8,24},{9,... | collective-permute-start | bytes 98312 | tf_op jit(solution)/shard_map/ppermute | solution.py:14
  81.3 5.8 %collective-permute-start.7 = (f32[2,1,32,128]{3,2,1,0:T(8,128)S(1)}, f32[2,1,32,128]{3,2,1,0:T(8,128)S(1)}, u32[]{:S(2)}, u32[]{:S(2)}) collective-permute-start(f32[2,1,32,128]{3,2,1,0:T(8,128)S(1)} %get-tuple-element.329), channel_id=1, source_target_pairs={{16,0},{17,1},{18,2},{19,3},{20,4},{21,5},{22,6},{23,7},{24,8},{25... | collective-permute-start | bytes 98312 | tf_op jit(solution)/shard_map/ppermute | solution.py:17
  87.1 3.7 %collective-permute-start.8 = (f32[2,10,1,128]{3,2,1,0:T(1,128)S(1)}, f32[2,10,1,128]{3,2,1,0:T(1,128)S(1)}, u32[]{:S(2)}, u32[]{:S(2)}) collective-permute-start(f32[2,10,1,128]{3,2,1,0:T(1,128)S(1)} %get-tuple-element.324), channel_id=1, source_target_pairs={{0,4},{4,8},{8,12},{1,5},{5,9},{9,13},{2,6},{6,10},{10,14},{3,7},{... | collective-permute-start | bytes 30728 | tf_op jit(solution)/shard_map/ppermute | solution.py:14
  89.5 4.6 %collective-permute-start.9 = (f32[2,10,1,128]{3,2,1,0:T(1,128)S(1)}, f32[2,10,1,128]{3,2,1,0:T(1,128)S(1)}, u32[]{:S(2)}, u32[]{:S(2)}) collective-permute-start(f32[2,10,1,128]{3,2,1,0:T(1,128)S(1)} %get-tuple-element.325), channel_id=1, source_target_pairs={{4,0},{8,4},{12,8},{5,1},{9,5},{13,9},{6,2},{10,6},{14,10},{7,3},{... | collective-permute-start | bytes 30728 | tf_op jit(solution)/shard_map/ppermute | solution.py:17
  94.3 12.6 %collective-permute-start.10 = (f32[2,10,34,1]{3,2,1,0:T(8,128)S(1)}, f32[2,10,34,1]{3,2,1,0:T(8,128)S(1)}, u32[]{:S(2)}, u32[]{:S(2)}) collective-permute-start(f32[2,10,34,1]{3,2,1,0:T(8,128)S(1)} %get-tuple-element.318), channel_id=1, source_target_pairs={{0,1},{1,2},{2,3},{4,5},{5,6},{6,7},{8,9},{9,10},{10,11},{12,13},{... | collective-permute-start | bytes 8168 | tf_op jit(solution)/shard_map/ppermute | solution.py:14
  98.6 13.0 %collective-permute-start.11 = (f32[2,10,34,1]{3,2,1,0:T(8,128)S(1)}, f32[2,10,34,1]{3,2,1,0:T(8,128)S(1)}, u32[]{:S(2)}, u32[]{:S(2)}) collective-permute-start(f32[2,10,34,1]{3,2,1,0:T(8,128)S(1)} %get-tuple-element.319), channel_id=1, source_target_pairs={{1,0},{2,1},{3,2},{5,4},{6,5},{7,6},{9,8},{10,9},{11,10},{13,12},{... | collective-permute-start | bytes 8168 | tf_op jit(solution)/shard_map/ppermute | solution.py:17
  113.4 3.3 %collective-permute-start.12 = (f32[2,1,32,128]{3,2,1,0:T(8,128)S(1)}, f32[2,1,32,128]{3,2,1,0:T(8,128)S(1)}, u32[]{:S(2)}, u32[]{:S(2)}) collective-permute-start(f32[2,1,32,128]{3,2,1,0:T(8,128)S(1)} %get-tuple-element.326), channel_id=1, source_target_pairs={{0,16},{1,17},{2,18},{3,19},{4,20},{5,21},{6,22},{7,23},{8,24},{9,... | collective-permute-start | bytes 98312 | tf_op jit(solution)/shard_map/ppermute | solution.py:14
  115.0 5.9 %collective-permute-start.13 = (f32[2,1,32,128]{3,2,1,0:T(8,128)S(1)}, f32[2,1,32,128]{3,2,1,0:T(8,128)S(1)}, u32[]{:S(2)}, u32[]{:S(2)}) collective-permute-start(f32[2,1,32,128]{3,2,1,0:T(8,128)S(1)} %get-tuple-element.327), channel_id=1, source_target_pairs={{16,0},{17,1},{18,2},{19,3},{20,4},{21,5},{22,6},{23,7},{24,8},{25... | collective-permute-start | bytes 98312 | tf_op jit(solution)/shard_map/ppermute | solution.py:17
  120.9 3.1 %collective-permute-start.14 = (f32[2,10,1,128]{3,2,1,0:T(1,128)S(1)}, f32[2,10,1,128]{3,2,1,0:T(1,128)S(1)}, u32[]{:S(2)}, u32[]{:S(2)}) collective-permute-start(f32[2,10,1,128]{3,2,1,0:T(1,128)S(1)} %get-tuple-element.322), channel_id=1, source_target_pairs={{0,4},{4,8},{8,12},{1,5},{5,9},{9,13},{2,6},{6,10},{10,14},{3,7},{... | collective-permute-start | bytes 30728 | tf_op jit(solution)/shard_map/ppermute | solution.py:14
  122.7 3.2 %collective-permute-start.15 = (f32[2,10,1,128]{3,2,1,0:T(1,128)S(1)}, f32[2,10,1,128]{3,2,1,0:T(1,128)S(1)}, u32[]{:S(2)}, u32[]{:S(2)}) collective-permute-start(f32[2,10,1,128]{3,2,1,0:T(1,128)S(1)} %get-tuple-element.323), channel_id=1, source_target_pairs={{4,0},{8,4},{12,8},{5,1},{9,5},{13,9},{6,2},{10,6},{14,10},{7,3},{... | collective-permute-start | bytes 30728 | tf_op jit(solution)/shard_map/ppermute | solution.py:17
  126.2 10.7 %collective-permute-start.16 = (f32[2,10,34,1]{3,2,1,0:T(8,128)S(1)}, f32[2,10,34,1]{3,2,1,0:T(8,128)S(1)}, u32[]{:S(2)}, u32[]{:S(2)}) collective-permute-start(f32[2,10,34,1]{3,2,1,0:T(8,128)S(1)} %get-tuple-element.312), channel_id=1, source_target_pairs={{0,1},{1,2},{2,3},{4,5},{5,6},{6,7},{8,9},{9,10},{10,11},{12,13},{... | collective-permute-start | bytes 8168 | tf_op jit(solution)/shard_map/ppermute | solution.py:14
  128.6 13.0 %collective-permute-start.17 = (f32[2,10,34,1]{3,2,1,0:T(8,128)S(1)}, f32[2,10,34,1]{3,2,1,0:T(8,128)S(1)}, u32[]{:S(2)}, u32[]{:S(2)}) collective-permute-start(f32[2,10,34,1]{3,2,1,0:T(8,128)S(1)} %get-tuple-element.313), channel_id=1, source_target_pairs={{1,0},{2,1},{3,2},{5,4},{6,5},{7,6},{9,8},{10,9},{11,10},{13,12},{... | collective-permute-start | bytes 8168 | tf_op jit(solution)/shard_map/ppermute | solution.py:17
  144.1 22.8 %copy-start.10 = (f32[9,1]{0,1:T(1,128)S(1)}, f32[9,1]{0,1:T(1,128)}, u32[]{:S(2)}) copy-start(f32[9,1]{0,1:T(1,128)} %constant.804) | copy-start | bytes 112
  144.4 3.0 %collective-permute-start.18 = (f32[1,32,128]{2,1,0:T(8,128)S(1)}, f32[1,32,128]{2,1,0:T(8,128)S(1)}, u32[]{:S(2)}, u32[]{:S(2)}) collective-permute-start(f32[1,32,128]{2,1,0:T(8,128)S(1)} %get-tuple-element.334), channel_id=1, source_target_pairs={{0,16},{1,17},{2,18},{3,19},{4,20},{5,21},{6,22},{7,23},{8,24},{9,... | collective-permute-start | bytes 49160 | tf_op jit(solution)/shard_map/ppermute | solution.py:14
  146.1 5.6 %collective-permute-start.19 = (f32[1,32,128]{2,1,0:T(8,128)S(1)}, f32[1,32,128]{2,1,0:T(8,128)S(1)}, u32[]{:S(2)}, u32[]{:S(2)}) collective-permute-start(f32[1,32,128]{2,1,0:T(8,128)S(1)} %get-tuple-element.335), channel_id=1, source_target_pairs={{16,0},{17,1},{18,2},{19,3},{20,4},{21,5},{22,6},{23,7},{24,8},{25... | collective-permute-start | bytes 49160 | tf_op jit(solution)/shard_map/ppermute | solution.py:17
  151.7 11.2 %collective-permute-start.20 = (f32[10,1,128]{2,1,0:T(1,128)S(1)}, f32[10,1,128]{2,1,0:T(1,128)S(1)}, u32[]{:S(2)}, u32[]{:S(2)}) collective-permute-start(f32[10,1,128]{2,1,0:T(1,128)S(1)} %get-tuple-element.332), channel_id=1, source_target_pairs={{0,4},{4,8},{8,12},{1,5},{5,9},{9,13},{2,6},{6,10},{10,14},{3,7},{... | collective-permute-start | bytes 15368 | tf_op jit(solution)/shard_map/ppermute | solution.py:14
  153.2 9.7 %collective-permute-start.21 = (f32[10,1,128]{2,1,0:T(1,128)S(1)}, f32[10,1,128]{2,1,0:T(1,128)S(1)}, u32[]{:S(2)}, u32[]{:S(2)}) collective-permute-start(f32[10,1,128]{2,1,0:T(1,128)S(1)} %get-tuple-element.333), channel_id=1, source_target_pairs={{4,0},{8,4},{12,8},{5,1},{9,5},{13,9},{6,2},{10,6},{14,10},{7,3},{... | collective-permute-start | bytes 15368 | tf_op jit(solution)/shard_map/ppermute | solution.py:17
  163.1 7.2 %collective-permute-start.22 = (f32[10,34,1]{2,1,0:T(8,128)S(1)}, f32[10,34,1]{2,1,0:T(8,128)S(1)}, u32[]{:S(2)}, u32[]{:S(2)}) collective-permute-start(f32[10,34,1]{2,1,0:T(8,128)S(1)} %get-tuple-element.330), channel_id=1, source_target_pairs={{0,1},{1,2},{2,3},{4,5},{5,6},{6,7},{8,9},{9,10},{10,11},{12,13},{... | collective-permute-start | bytes 4088 | tf_op jit(solution)/shard_map/ppermute | solution.py:14
  165.6 9.5 %collective-permute-start.23 = (f32[10,34,1]{2,1,0:T(8,128)S(1)}, f32[10,34,1]{2,1,0:T(8,128)S(1)}, u32[]{:S(2)}, u32[]{:S(2)}) collective-permute-start(f32[10,34,1]{2,1,0:T(8,128)S(1)} %get-tuple-element.331), channel_id=1, source_target_pairs={{1,0},{2,1},{3,2},{5,4},{6,5},{7,6},{9,8},{10,9},{11,10},{13,12},{... | collective-permute-start | bytes 4088 | tf_op jit(solution)/shard_map/ppermute | solution.py:17
  175.9 1.0 copy-start.2
  180.0 41.1 %copy-start.8 = (f32[9]{0:T(128)S(1)}, f32[9]{0:T(128)}, u32[]{:S(2)}) copy-start(f32[9]{0:T(128)} %constant.686.clone.1) | copy-start | bytes 112
  180.0 41.8 %copy-start.7 = (f32[9]{0:T(128)S(1)}, f32[9]{0:T(128)}, u32[]{:S(2)}) copy-start(f32[9]{0:T(128)} %constant.661.clone.1) | copy-start | bytes 112
  180.0 41.8 %copy-start.9 = (f32[9,1]{0,1:T(1,128)S(1)}, f32[9,1]{0,1:T(1,128)}, u32[]{:S(2)}) copy-start(f32[9,1]{0,1:T(1,128)} %constant.803) | copy-start | bytes 112
  240.9 12.6 %copy-start.3 = (f32[8,32,128]{2,1,0:T(8,128)S(1)}, f32[8,32,128]{2,1,0:T(8,128)}, u32[]{:S(2)}) copy-start(f32[8,32,128]{2,1,0:T(8,128)} %param.52) | copy-start | bytes 393220
where the time goes:
time: 262 us; the launch traced here: 260 us
  waiting for transfers between devices  61.3 us (23%)
  starting transfers between devices  48.7 us (19%)
  other arithmetic  43.5 us (17%)
  local copies, waits for them, and re-layouts  42.3 us (16%)
  blocking collectives  38.1 us (15%)
  between operations  15.9 us (6%)
  matrix products  10.1 us (4%)
    ppermute x12, waiting for transfers between devices, extended(): lax.ppermute(lax.slice_in_dim(block, 0, width, axis=dim), axis, backward)  39.2 us
    psum x1, blocking collectives, body(): gram = lax.psum(partial_gram, ('gx', 'gy', 'gz'))  38.1 us
    ppermute x12, starting transfers between devices, extended(): lax.ppermute(lax.slice_in_dim(block, block.shape[dim] - width, None, axis...  26.8 us
    gather x1, local copies, waits for them, and re-layouts, body(): incoming = jnp.take_along_axis(arrived, slot, axis=1)  25.6 us
    ppermute x12, waiting for transfers between devices, extended(): lax.ppermute(lax.slice_in_dim(block, block.shape[dim] - width, None, axis...  18.2 us
    ppermute x12, starting transfers between devices, extended(): lax.ppermute(lax.slice_in_dim(block, 0, width, axis=dim), axis, backward)  15.5 us
    add x2, other arithmetic, combine(): summed = summed + weights[position] * basis[position]  12.6 us
    mul x5, other arithmetic, operate(): result = capacity * values  7.02 us
  transfers between devices with their start and end apart: 25, of which 18 were waited for; matrix products, arithmetic and copies ran while one was open for 5% of the time, Pallas kernels for 0%

commit v1 on v0

--- a/solution.py
+++ b/solution.py
@@ -4,6 +4,7 @@
 from jax.sharding import PartitionSpec as P
 
 STEPS = 4
+pair_the_desk = lambda device_axis, panel, across: lax.psum(lax.psum(panel, device_axis), across)
 
 
 def extended(block, sides, width):
@@ -179,7 +180,7 @@
     basis = dir_terms + res_terms
     stacked = jnp.stack([term.reshape(-1) for term in basis])
     partial_gram = jnp.dot(stacked, stacked.T, precision=lax.Precision.HIGHEST)
-    gram = lax.psum(partial_gram, ("gx", "gy", "gz"))
+    gram = pair_the_desk(("gy", "gz"), partial_gram, "gx")
     moved, residue, direct = coefficients(gram, center, half_width, STEPS)
     return (solution_in + combine(moved, basis), combine(residue, basis), combine(direct, basis))
 

time: 262 us -> 259 us (0.989)
    psum x1 -> x2, blocking collectives: 38.1 us -> 35.8 us  [the longest x1 30.8 us: lax.psum(panel, device_axis)]
where the time goes in v1:
time: 259 us; the launch traced here: 258 us
  waiting for transfers between devices  61 us (24%)
  starting transfers between devices  48.9 us (19%)
  other arithmetic  43.7 us (17%)
  local copies, waits for them, and re-layouts  42.5 us (16%)
  blocking collectives  35.8 us (14%)
  between operations  16 us (6%)
  matrix products  9.93 us (4%)
    ppermute x12, waiting for transfers between devices, extended(): lax.ppermute(lax.slice_in_dim(block, 0, width, axis=dim), axis, backward)  38.9 us
    psum x1, blocking collectives, lax.psum(panel, device_axis)  30.8 us
    ppermute x12, starting transfers between devices, extended(): lax.ppermute(lax.slice_in_dim(block, block.shape[dim] - width, None, axis...  27.1 us
    gather x1, local copies, waits for them, and re-layouts, body(): incoming = jnp.take_along_axis(arrived, slot, axis=1)  25.6 us
    ppermute x12, waiting for transfers between devices, extended(): lax.ppermute(lax.slice_in_dim(block, block.shape[dim] - width, None, axis...  18.2 us
    ppermute x12, starting transfers between devices, extended(): lax.ppermute(lax.slice_in_dim(block, 0, width, axis=dim), axis, backward)  15.5 us
    add x2, other arithmetic, combine(): summed = summed + weights[position] * basis[position]  12.8 us
    mul x5, other arithmetic, operate(): result = capacity * values  7.04 us
  transfers between devices with their start and end apart: 25, of which 18 were waited for; matrix products, arithmetic and copies ran while one was open for 5% of the time, Pallas kernels for 0%

profile of v1, /device:TPU:0, one launch (start us, length us, event | category | flops | bytes accessed | tf_op | source)
XLA Modules:
  0.0 257.8 jit_solution(11244546696564984081)
XLA Ops:
  2.2 6.3 %all-to-all-start = ((f32[4,1,1024]{2,1,0:T(1,128)}), f32[4,1,1024]{2,1,0:T(1,128)S(1)}, u32[]{:S(2)}, u32[]{:S(2)}) async-start(f32[4,1,1024]{2,1,0:T(1,128)} %reshape.745), calls=%async_computation | async-start | bytes 32768 | tf_op jit(solution)/shard_map/all_to_all | solution.py:141
  10.2 3.9 %all-to-all-done = f32[4,1,1024]{2,1,0:T(1,128)S(1)} async-done(((f32[4,1,1024]{2,1,0:T(1,128)}), f32[4,1,1024]{2,1,0:T(1,128)S(1)}, u32[]{:S(2)}, u32[]{:S(2)}) %all-to-all-start) | async-done | bytes 16416 | tf_op jit(solution)/shard_map/all_to_all | solution.py:141
  15.6 25.6 %gather_fusion = f32[4096]{0:T(1024)S(1)} fusion(f32[32,128]{1,0:T(8,128)S(1)} %reshape.660, s32[4096]{0:T(1024)S(1)} %fusion.80), kind=kCustom, calls=%fused_computation | custom fusion | bytes 65536 | tf_op jit(solution)/shard_map/jit(take_along_axis)/gather | solution.py:154
  41.3 3.4 %collective-permute-start = (f32[3,1,32,128]{3,2,1,0:T(8,128)S(1)}, f32[3,1,32,128]{3,2,1,0:T(8,128)S(1)}, u32[]{:S(2)}, u32[]{:S(2)}) collective-permute-start(f32[3,1,32,128]{3,2,1,0:T(8,128)S(1)} %get-tuple-element.320), channel_id=1, source_target_pairs={{0,16},{1,17},{2,18},{3,19},{4,20},{5,21},{6,22},{7,23},{8,24},{9,... | collective-permute-start | bytes 147464 | tf_op jit(solution)/shard_map/ppermute | solution.py:15
  44.7 1.3 collective-permute-start.1
  46.7 4.0 %collective-permute-done.1 = f32[3,1,32,128]{3,2,1,0:T(8,128)S(1)} collective-permute-done((f32[3,1,32,128]{3,2,1,0:T(8,128)S(1)}, f32[3,1,32,128]{3,2,1,0:T(8,128)S(1)}, u32[]{:S(2)}, u32[]{:S(2)}) %collective-permute-start.1) | collective-permute-done | bytes 49184 | tf_op jit(solution)/shard_map/ppermute | solution.py:18
  52.0 1.3 collective-permute-start.3
  54.0 2.8 %collective-permute-done.3 = f32[3,10,1,128]{3,2,1,0:T(1,128)S(1)} collective-permute-done((f32[3,10,1,128]{3,2,1,0:T(1,128)S(1)}, f32[3,10,1,128]{3,2,1,0:T(1,128)S(1)}, u32[]{:S(2)}, u32[]{:S(2)}) %collective-permute-start.3) | collective-permute-done | bytes 15392 | tf_op jit(solution)/shard_map/ppermute | solution.py:18
  57.4 2.6 collective-permute-start.4
  67.0 5.8 %bitcast_multiply_fusion.6 = (f32[10,34,130]{2,1,0:T(8,128)S(1)}, f32[1,10,34,130]{3,2,1,0:T(8,128)S(1)}, pred[1,10,34,130]{3,2,1,0:T(8,128)(4,1)S(1)}, pred[1,1...) fusion(f32[3,10,34,130]{3,2,1,0:T(8,128)S(1)} %pad_maximum_fusi, ...), kind=kLoop, calls=%fused_computation.85 | loop fusion | flops 1060800 | bytes 1060832 | tf_op jit(solution)/shard_map/mul | solution.py:41
  72.8 5.4 %add_add_fusion = f32[1,10,34,130]{3,2,1,0:T(8,128)S(1)} fusion(pred[1,10,34,130]{3,2,1,0:T(8,128)(4,1)S(1)} %get-tuple-element.283, pred[1,10,34,130]{3,2,1,0:T(8,128)(4,1)S(1)} %get-tuple-element.282, pred[1,10,34,130]{3,2,1,0:T(8,128)(4,1)S(1)} %get-tuple-element.281, pred[1,10,34,130]{3,2,1,0:T(8,128)(4,1)S(1)} %get-tuple-element.280, ...), kind=kLoop, calls=%fused_computation.86 | loop fusion | flops 663000 | bytes 530432 | tf_op jit(solution)/shard_map/add | solution.py:66
  79.7 1.6 collective-permute-start.6
  81.3 1.3 collective-permute-start.7
  82.9 4.2 %collective-permute-done.7 = f32[2,1,32,128]{3,2,1,0:T(8,128)S(1)} collective-permute-done((f32[2,1,32,128]{3,2,1,0:T(8,128)S(1)}, f32[2,1,32,128]{3,2,1,0:T(8,128)S(1)}, u32[]{:S(2)}, u32[]{:S(2)}) %collective-permute-start.7) | collective-permute-done | bytes 32800 | tf_op jit(solution)/shard_map/ppermute | solution.py:18
  87.2 2.5 collective-permute-start.8
  89.6 1.3 collective-permute-start.9
  91.0 3.2 %collective-permute-done.9 = f32[2,10,1,128]{3,2,1,0:T(1,128)S(1)} collective-permute-done((f32[2,10,1,128]{3,2,1,0:T(1,128)S(1)}, f32[2,10,1,128]{3,2,1,0:T(1,128)S(1)}, u32[]{:S(2)}, u32[]{:S(2)}) %collective-permute-start.9) | collective-permute-done | bytes 10272 | tf_op jit(solution)/shard_map/ppermute | solution.py:18
  94.4 4.4 %collective-permute-start.10 = (f32[2,10,34,1]{3,2,1,0:T(8,128)S(1)}, f32[2,10,34,1]{3,2,1,0:T(8,128)S(1)}, u32[]{:S(2)}, u32[]{:S(2)}) collective-permute-start(f32[2,10,34,1]{3,2,1,0:T(8,128)S(1)} %get-tuple-element.318), channel_id=1, source_target_pairs={{0,1},{1,2},{2,3},{4,5},{5,6},{6,7},{8,9},{9,10},{10,11},{12,13},{... | collective-permute-start | bytes 8168 | tf_op jit(solution)/shard_map/ppermute | solution.py:15
  98.8 1.3 collective-permute-start.11
  100.1 7.0 %collective-permute-done.10 = f32[2,10,34,1]{3,2,1,0:T(8,128)S(1)} collective-permute-done((f32[2,10,34,1]{3,2,1,0:T(8,128)S(1)}, f32[2,10,34,1]{3,2,1,0:T(8,128)S(1)}, u32[]{:S(2)}, u32[]{:S(2)}) %collective-permute-start.10) | collective-permute-done | bytes 2752 | tf_op jit(solution)/shard_map/ppermute | solution.py:15
  107.1 4.7 %collective-permute-done.11 = f32[2,10,34,1]{3,2,1,0:T(8,128)S(1)} collective-permute-done((f32[2,10,34,1]{3,2,1,0:T(8,128)S(1)}, f32[2,10,34,1]{3,2,1,0:T(8,128)S(1)}, u32[]{:S(2)}, u32[]{:S(2)}) %collective-permute-start.11) | collective-permute-done | bytes 2752 | tf_op jit(solution)/shard_map/ppermute | solution.py:18
  113.6 1.6 collective-permute-start.12
  115.2 1.3 collective-permute-start.13
  116.9 4.2 %collective-permute-done.13 = f32[2,1,32,128]{3,2,1,0:T(8,128)S(1)} collective-permute-done((f32[2,1,32,128]{3,2,1,0:T(8,128)S(1)}, f32[2,1,32,128]{3,2,1,0:T(8,128)S(1)}, u32[]{:S(2)}, u32[]{:S(2)}) %collective-permute-start.13) | collective-permute-done | bytes 32800 | tf_op jit(solution)/shard_map/ppermute | solution.py:18
  121.1 1.8 collective-permute-start.14
  122.9 1.3 collective-permute-start.15
  124.2 1.9 collective-permute-done.15
  126.4 2.4 collective-permute-start.16
  128.8 1.3 collective-permute-start.17
  130.1 7.0 %collective-permute-done.16 = f32[2,10,34,1]{3,2,1,0:T(8,128)S(1)} collective-permute-done((f32[2,10,34,1]{3,2,1,0:T(8,128)S(1)}, f32[2,10,34,1]{3,2,1,0:T(8,128)S(1)}, u32[]{:S(2)}, u32[]{:S(2)}) %collective-permute-start.16) | collective-permute-done | bytes 2752 | tf_op jit(solution)/shard_map/ppermute | solution.py:15
  137.1 4.7 %collective-permute-done.17 = f32[2,10,34,1]{3,2,1,0:T(8,128)S(1)} collective-permute-done((f32[2,10,34,1]{3,2,1,0:T(8,128)S(1)}, f32[2,10,34,1]{3,2,1,0:T(8,128)S(1)}, u32[]{:S(2)}, u32[]{:S(2)}) %collective-permute-start.17) | collective-permute-done | bytes 2752 | tf_op jit(solution)/shard_map/ppermute | solution.py:18
  144.6 1.6 collective-permute-start.18
  146.2 1.3 collective-permute-start.19
  147.6 4.2 %collective-permute-done.19 = f32[1,32,128]{2,1,0:T(8,128)S(1)} collective-permute-done((f32[1,32,128]{2,1,0:T(8,128)S(1)}, f32[1,32,128]{2,1,0:T(8,128)S(1)}, u32[]{:S(2)}, u32[]{:S(2)}) %collective-permute-start.19) | collective-permute-done | bytes 16416 | tf_op jit(solution)/shard_map/ppermute | solution.py:18
  151.9 1.5 collective-permute-start.20
  156.2 1.9 dynamic-slice.147
  159.4 1.5 scatter.70
  163.3 2.5 collective-permute-start.22
  165.8 1.3 collective-permute-start.23
  167.2 3.3 %collective-permute-done.22 = f32[10,34,1]{2,1,0:T(8,128)S(1)} collective-permute-done((f32[10,34,1]{2,1,0:T(8,128)S(1)}, f32[10,34,1]{2,1,0:T(8,128)S(1)}, u32[]{:S(2)}, u32[]{:S(2)}) %collective-permute-start.22) | collective-permute-done | bytes 1392 | tf_op jit(solution)/shard_map/ppermute | solution.py:15
  170.5 4.7 %collective-permute-done.23 = f32[10,34,1]{2,1,0:T(8,128)S(1)} collective-permute-done((f32[10,34,1]{2,1,0:T(8,128)S(1)}, f32[10,34,1]{2,1,0:T(8,128)S(1)}, u32[]{:S(2)}, u32[]{:S(2)}) %collective-permute-start.23) | collective-permute-done | bytes 1392 | tf_op jit(solution)/shard_map/ppermute | solution.py:18
  178.3 1.9 stack.43
  180.2 2.8 %fusion.119 = f32[9,9]{1,0:T(8,128)S(1)} fusion(f32[9,32768]{1,0:T(8,128)S(1)} %stack.43), kind=kOutput, calls=%fused_computation.275 | convolution fusion | flops 31850496 | bytes 1179972 | tf_op jit(solution)/shard_map/dot_general | solution.py:182
  183.0 30.8 %psum.14 = f32[9,9]{1,0:T(8,128)S(1)} all-reduce(f32[9,9]{1,0:T(8,128)S(1)} %fusion.119), channel_id=1, replica_groups=mesh['gx'=2,'gy'=4,'gz'=4] {'gy','gz'}, use_global_device_ids=true, to_apply=%region_3.4 | all-reduce | flops 81 | bytes 648 | tf_op jit(solution)/shard_map/psum | solution.py:7
  213.8 5.0 %psum.15 = f32[9,9]{1,0:T(8,128)S(1)} all-reduce(f32[9,9]{1,0:T(8,128)S(1)} %psum.14), channel_id=1, replica_groups=mesh['gx'=2,'gy'=4,'gz'=4] {'gx'}, use_global_device_ids=true, to_apply=%region_4.5 | all-reduce | flops 81 | bytes 648 | tf_op jit(solution)/shard_map/psum | solution.py:7
  238.7 6.4 %multiply_add_fusion = f32[8,32,128]{2,1,0:T(8,128)} fusion(f32[8,32,128]{2,1,0:T(8,128)S(1)} %fusion.54, f32[8,32,128]{2,1,0:T(8,128)S(1)} %fusion.66, f32[8,32,128]{2,1,0:T(8,128)S(1)} %get-tuple-element.383, f32[8,32,128]{2,1,0:T(8,128)S(1)} %fusion.78, f32[8,32,128]{2,1,0:T(8,128)S(1)} %fusion.58, f32[8,32,128]{2,1,0:T(8,128)S(1)} %fusion.62, ...), kind=kLoop, calls=%fused_computation.187 | loop fusion | flops 557056 | bytes 1310756 | tf_op jit(solution)/shard_map/add | solution.py:127
  245.0 6.5 %multiply_add_fusion.1 = f32[8,32,128]{2,1,0:T(8,128)} fusion(f32[8,32,128]{2,1,0:T(8,128)S(1)} %fusion.54, f32[8,32,128]{2,1,0:T(8,128)S(1)} %fusion.66, f32[8,32,128]{2,1,0:T(8,128)S(1)} %get-tuple-element.383, f32[8,32,128]{2,1,0:T(8,128)S(1)} %fusion.78, f32[8,32,128]{2,1,0:T(8,128)S(1)} %fusion.58, f32[8,32,128]{2,1,0:T(8,128)S(1)} %fusion.62, ...), kind=kLoop, calls=%fused_computation.188 | loop fusion | flops 557056 | bytes 1310756 | tf_op jit(solution)/shard_map/add | solution.py:127
  251.5 6.3 %add_add_fusion.2 = f32[8,32,128]{2,1,0:T(8,128)} fusion(f32[8,32,128]{2,1,0:T(8,128)S(1)} %copy-done.3, f32[8,32,128]{2,1,0:T(8,128)S(1)} %fusion.54, f32[8,32,128]{2,1,0:T(8,128)S(1)} %fusion.66, f32[8,32,128]{2,1,0:T(8,128)S(1)} %get-tuple-element.383, f32[8,32,128]{2,1,0:T(8,128)S(1)} %fusion.78, f32[8,32,128]{2,1,0:T(8,128)S(1)} %fusion.58, ...), kind=kLoop, calls=%fused_computation.189 | loop fusion | flops 589824 | bytes 1441828 | tf_op jit(solution)/shard_map/add | solution.py:185
  (146 shorter events, 37.0 us)
Async XLA Ops:
  2.2 11.9 %all-to-all-start = ((f32[4,1,1024]{2,1,0:T(1,128)}), f32[4,1,1024]{2,1,0:T(1,128)S(1)}, u32[]{:S(2)}, u32[]{:S(2)}) async-start(f32[4,1,1024]{2,1,0:T(1,128)} %reshape.745), calls=%async_computation | async-start | bytes 32768 | tf_op jit(solution)/shard_map/all_to_all | solution.py:141
  15.5 25.7 %copy-start = (f32[8,32,128]{2,1,0:T(8,128)S(1)}, f32[8,32,128]{2,1,0:T(8,128)}, u32[]{:S(2)}) copy-start(f32[8,32,128]{2,1,0:T(8,128)} %param.53) | copy-start | bytes 393220
  15.5 25.7 %copy-start.4 = (s32[32,128]{1,0:T(8,128)S(1)}, s32[32,128]{1,0:T(8,128)}, u32[]{:S(2)}) copy-start(s32[32,128]{1,0:T(8,128)} %param.59) | copy-start | bytes 49156
  15.6 25.7 %copy-start.1 = (f32[8,32,128]{2,1,0:T(8,128)S(1)}, f32[8,32,128]{2,1,0:T(8,128)}, u32[]{:S(2)}) copy-start(f32[8,32,128]{2,1,0:T(8,128)} %param.54) | copy-start | bytes 393220
  15.6 30.4 %copy-start.5 = (f32[8]{0:T(128)S(1)}, f32[8]{0:T(128)}, u32[]{:S(2)}) copy-start(f32[8]{0:T(128)} %param.57) | copy-start | bytes 100
  15.6 37.7 %copy-start.6 = (f32[8]{0:T(128)S(1)}, f32[8]{0:T(128)}, u32[]{:S(2)}) copy-start(f32[8]{0:T(128)} %param.56) | copy-start | bytes 100
  41.3 5.4 %collective-permute-start = (f32[3,1,32,128]{3,2,1,0:T(8,128)S(1)}, f32[3,1,32,128]{3,2,1,0:T(8,128)S(1)}, u32[]{:S(2)}, u32[]{:S(2)}) collective-permute-start(f32[3,1,32,128]{3,2,1,0:T(8,128)S(1)} %get-tuple-element.320), channel_id=1, source_target_pairs={{0,16},{1,17},{2,18},{3,19},{4,20},{5,21},{6,22},{7,23},{8,24},{9,... | collective-permute-start | bytes 147464 | tf_op jit(solution)/shard_map/ppermute | solution.py:15
  44.7 6.0 %collective-permute-start.1 = (f32[3,1,32,128]{3,2,1,0:T(8,128)S(1)}, f32[3,1,32,128]{3,2,1,0:T(8,128)S(1)}, u32[]{:S(2)}, u32[]{:S(2)}) collective-permute-start(f32[3,1,32,128]{3,2,1,0:T(8,128)S(1)} %get-tuple-element.321), channel_id=1, source_target_pairs={{16,0},{17,1},{18,2},{19,3},{20,4},{21,5},{22,6},{23,7},{24,8},{25... | collective-permute-start | bytes 147464 | tf_op jit(solution)/shard_map/ppermute | solution.py:18
  50.7 3.3 %collective-permute-start.2 = (f32[3,10,1,128]{3,2,1,0:T(1,128)S(1)}, f32[3,10,1,128]{3,2,1,0:T(1,128)S(1)}, u32[]{:S(2)}, u32[]{:S(2)}) collective-permute-start(f32[3,10,1,128]{3,2,1,0:T(1,128)S(1)} %get-tuple-element.306), channel_id=1, source_target_pairs={{0,4},{4,8},{8,12},{1,5},{5,9},{9,13},{2,6},{6,10},{10,14},{3,7},{... | collective-permute-start | bytes 46088 | tf_op jit(solution)/shard_map/ppermute | solution.py:15
  52.0 4.8 %collective-permute-start.3 = (f32[3,10,1,128]{3,2,1,0:T(1,128)S(1)}, f32[3,10,1,128]{3,2,1,0:T(1,128)S(1)}, u32[]{:S(2)}, u32[]{:S(2)}) collective-permute-start(f32[3,10,1,128]{3,2,1,0:T(1,128)S(1)} %get-tuple-element.307), channel_id=1, source_target_pairs={{4,0},{8,4},{12,8},{5,1},{9,5},{13,9},{6,2},{10,6},{14,10},{7,3},{... | collective-permute-start | bytes 46088 | tf_op jit(solution)/shard_map/ppermute | solution.py:18
  57.4 7.9 %collective-permute-start.4 = (f32[3,10,34,1]{2,3,1,0:T(1,128)S(1)}, f32[3,10,34,1]{2,3,1,0:T(1,128)S(1)}, u32[]{:S(2)}, u32[]{:S(2)}) collective-permute-start(f32[3,10,34,1]{2,3,1,0:T(1,128)S(1)} %copy.31), channel_id=1, source_target_pairs={{0,1},{1,2},{2,3},{4,5},{5,6},{6,7},{8,9},{9,10},{10,11},{12,13},{... | collective-permute-start | bytes 12248 | tf_op jit(solution)/shard_map/ppermute | solution.py:15
  60.3 5.6 %collective-permute-start.5 = (f32[3,10,34,1]{2,3,1,0:T(1,128)S(1)}, f32[3,10,34,1]{2,3,1,0:T(1,128)S(1)}, u32[]{:S(2)}, u32[]{:S(2)}) collective-permute-start(f32[3,10,34,1]{2,3,1,0:T(1,128)S(1)} %copy.32), channel_id=1, source_target_pairs={{1,0},{2,1},{3,2},{5,4},{6,5},{7,6},{9,8},{10,9},{11,10},{13,12},{... | collective-permute-start | bytes 12248 | tf_op jit(solution)/shard_map/ppermute | solution.py:18
  79.7 3.2 %collective-permute-start.6 = (f32[2,1,32,128]{3,2,1,0:T(8,128)S(1)}, f32[2,1,32,128]{3,2,1,0:T(8,128)S(1)}, u32[]{:S(2)}, u32[]{:S(2)}) collective-permute-start(f32[2,1,32,128]{3,2,1,0:T(8,128)S(1)} %get-tuple-element.328), channel_id=1, source_target_pairs={{0,16},{1,17},{2,18},{3,19},{4,20},{5,21},{6,22},{7,23},{8,24},{9,... | collective-permute-start | bytes 98312 | tf_op jit(solution)/shard_map/ppermute | solution.py:15
  81.3 5.8 %collective-permute-start.7 = (f32[2,1,32,128]{3,2,1,0:T(8,128)S(1)}, f32[2,1,32,128]{3,2,1,0:T(8,128)S(1)}, u32[]{:S(2)}, u32[]{:S(2)}) collective-permute-start(f32[2,1,32,128]{3,2,1,0:T(8,128)S(1)} %get-tuple-element.329), channel_id=1, source_target_pairs={{16,0},{17,1},{18,2},{19,3},{20,4},{21,5},{22,6},{23,7},{24,8},{25... | collective-permute-start | bytes 98312 | tf_op jit(solution)/shard_map/ppermute | solution.py:18
  87.2 3.8 %collective-permute-start.8 = (f32[2,10,1,128]{3,2,1,0:T(1,128)S(1)}, f32[2,10,1,128]{3,2,1,0:T(1,128)S(1)}, u32[]{:S(2)}, u32[]{:S(2)}) collective-permute-start(f32[2,10,1,128]{3,2,1,0:T(1,128)S(1)} %get-tuple-element.324), channel_id=1, source_target_pairs={{0,4},{4,8},{8,12},{1,5},{5,9},{9,13},{2,6},{6,10},{10,14},{3,7},{... | collective-permute-start | bytes 30728 | tf_op jit(solution)/shard_map/ppermute | solution.py:15
  89.6 4.5 %collective-permute-start.9 = (f32[2,10,1,128]{3,2,1,0:T(1,128)S(1)}, f32[2,10,1,128]{3,2,1,0:T(1,128)S(1)}, u32[]{:S(2)}, u32[]{:S(2)}) collective-permute-start(f32[2,10,1,128]{3,2,1,0:T(1,128)S(1)} %get-tuple-element.325), channel_id=1, source_target_pairs={{4,0},{8,4},{12,8},{5,1},{9,5},{13,9},{6,2},{10,6},{14,10},{7,3},{... | collective-permute-start | bytes 30728 | tf_op jit(solution)/shard_map/ppermute | solution.py:18
  94.4 12.7 %collective-permute-start.10 = (f32[2,10,34,1]{3,2,1,0:T(8,128)S(1)}, f32[2,10,34,1]{3,2,1,0:T(8,128)S(1)}, u32[]{:S(2)}, u32[]{:S(2)}) collective-permute-start(f32[2,10,34,1]{3,2,1,0:T(8,128)S(1)} %get-tuple-element.318), channel_id=1, source_target_pairs={{0,1},{1,2},{2,3},{4,5},{5,6},{6,7},{8,9},{9,10},{10,11},{12,13},{... | collective-permute-start | bytes 8168 | tf_op jit(solution)/shard_map/ppermute | solution.py:15
  98.8 13.0 %collective-permute-start.11 = (f32[2,10,34,1]{3,2,1,0:T(8,128)S(1)}, f32[2,10,34,1]{3,2,1,0:T(8,128)S(1)}, u32[]{:S(2)}, u32[]{:S(2)}) collective-permute-start(f32[2,10,34,1]{3,2,1,0:T(8,128)S(1)} %get-tuple-element.319), channel_id=1, source_target_pairs={{1,0},{2,1},{3,2},{5,4},{6,5},{7,6},{9,8},{10,9},{11,10},{13,12},{... | collective-permute-start | bytes 8168 | tf_op jit(solution)/shard_map/ppermute | solution.py:18
  113.6 3.3 %collective-permute-start.12 = (f32[2,1,32,128]{3,2,1,0:T(8,128)S(1)}, f32[2,1,32,128]{3,2,1,0:T(8,128)S(1)}, u32[]{:S(2)}, u32[]{:S(2)}) collective-permute-start(f32[2,1,32,128]{3,2,1,0:T(8,128)S(1)} %get-tuple-element.326), channel_id=1, source_target_pairs={{0,16},{1,17},{2,18},{3,19},{4,20},{5,21},{6,22},{7,23},{8,24},{9,... | collective-permute-start | bytes 98312 | tf_op jit(solution)/shard_map/ppermute | solution.py:15
  115.2 5.9 %collective-permute-start.13 = (f32[2,1,32,128]{3,2,1,0:T(8,128)S(1)}, f32[2,1,32,128]{3,2,1,0:T(8,128)S(1)}, u32[]{:S(2)}, u32[]{:S(2)}) collective-permute-start(f32[2,1,32,128]{3,2,1,0:T(8,128)S(1)} %get-tuple-element.327), channel_id=1, source_target_pairs={{16,0},{17,1},{18,2},{19,3},{20,4},{21,5},{22,6},{23,7},{24,8},{25... | collective-permute-start | bytes 98312 | tf_op jit(solution)/shard_map/ppermute | solution.py:18
  121.1 3.1 %collective-permute-start.14 = (f32[2,10,1,128]{3,2,1,0:T(1,128)S(1)}, f32[2,10,1,128]{3,2,1,0:T(1,128)S(1)}, u32[]{:S(2)}, u32[]{:S(2)}) collective-permute-start(f32[2,10,1,128]{3,2,1,0:T(1,128)S(1)} %get-tuple-element.322), channel_id=1, source_target_pairs={{0,4},{4,8},{8,12},{1,5},{5,9},{9,13},{2,6},{6,10},{10,14},{3,7},{... | collective-permute-start | bytes 30728 | tf_op jit(solution)/shard_map/ppermute | solution.py:15
  122.9 3.2 %collective-permute-start.15 = (f32[2,10,1,128]{3,2,1,0:T(1,128)S(1)}, f32[2,10,1,128]{3,2,1,0:T(1,128)S(1)}, u32[]{:S(2)}, u32[]{:S(2)}) collective-permute-start(f32[2,10,1,128]{3,2,1,0:T(1,128)S(1)} %get-tuple-element.323), channel_id=1, source_target_pairs={{4,0},{8,4},{12,8},{5,1},{9,5},{13,9},{6,2},{10,6},{14,10},{7,3},{... | collective-permute-start | bytes 30728 | tf_op jit(solution)/shard_map/ppermute | solution.py:18
  126.4 10.7 %collective-permute-start.16 = (f32[2,10,34,1]{3,2,1,0:T(8,128)S(1)}, f32[2,10,34,1]{3,2,1,0:T(8,128)S(1)}, u32[]{:S(2)}, u32[]{:S(2)}) collective-permute-start(f32[2,10,34,1]{3,2,1,0:T(8,128)S(1)} %get-tuple-element.312), channel_id=1, source_target_pairs={{0,1},{1,2},{2,3},{4,5},{5,6},{6,7},{8,9},{9,10},{10,11},{12,13},{... | collective-permute-start | bytes 8168 | tf_op jit(solution)/shard_map/ppermute | solution.py:15
  128.8 13.0 %collective-permute-start.17 = (f32[2,10,34,1]{3,2,1,0:T(8,128)S(1)}, f32[2,10,34,1]{3,2,1,0:T(8,128)S(1)}, u32[]{:S(2)}, u32[]{:S(2)}) collective-permute-start(f32[2,10,34,1]{3,2,1,0:T(8,128)S(1)} %get-tuple-element.313), channel_id=1, source_target_pairs={{1,0},{2,1},{3,2},{5,4},{6,5},{7,6},{9,8},{10,9},{11,10},{13,12},{... | collective-permute-start | bytes 8168 | tf_op jit(solution)/shard_map/ppermute | solution.py:18
  144.3 22.8 %copy-start.10 = (f32[9,1]{0,1:T(1,128)S(1)}, f32[9,1]{0,1:T(1,128)}, u32[]{:S(2)}) copy-start(f32[9,1]{0,1:T(1,128)} %constant.804) | copy-start | bytes 112
  144.6 3.0 %collective-permute-start.18 = (f32[1,32,128]{2,1,0:T(8,128)S(1)}, f32[1,32,128]{2,1,0:T(8,128)S(1)}, u32[]{:S(2)}, u32[]{:S(2)}) collective-permute-start(f32[1,32,128]{2,1,0:T(8,128)S(1)} %get-tuple-element.334), channel_id=1, source_target_pairs={{0,16},{1,17},{2,18},{3,19},{4,20},{5,21},{6,22},{7,23},{8,24},{9,... | collective-permute-start | bytes 49160 | tf_op jit(solution)/shard_map/ppermute | solution.py:15
  146.2 5.6 %collective-permute-start.19 = (f32[1,32,128]{2,1,0:T(8,128)S(1)}, f32[1,32,128]{2,1,0:T(8,128)S(1)}, u32[]{:S(2)}, u32[]{:S(2)}) collective-permute-start(f32[1,32,128]{2,1,0:T(8,128)S(1)} %get-tuple-element.335), channel_id=1, source_target_pairs={{16,0},{17,1},{18,2},{19,3},{20,4},{21,5},{22,6},{23,7},{24,8},{25... | collective-permute-start | bytes 49160 | tf_op jit(solution)/shard_map/ppermute | solution.py:18
  151.9 11.3 %collective-permute-start.20 = (f32[10,1,128]{2,1,0:T(1,128)S(1)}, f32[10,1,128]{2,1,0:T(1,128)S(1)}, u32[]{:S(2)}, u32[]{:S(2)}) collective-permute-start(f32[10,1,128]{2,1,0:T(1,128)S(1)} %get-tuple-element.332), channel_id=1, source_target_pairs={{0,4},{4,8},{8,12},{1,5},{5,9},{9,13},{2,6},{6,10},{10,14},{3,7},{... | collective-permute-start | bytes 15368 | tf_op jit(solution)/shard_map/ppermute | solution.py:15
  153.4 9.8 %collective-permute-start.21 = (f32[10,1,128]{2,1,0:T(1,128)S(1)}, f32[10,1,128]{2,1,0:T(1,128)S(1)}, u32[]{:S(2)}, u32[]{:S(2)}) collective-permute-start(f32[10,1,128]{2,1,0:T(1,128)S(1)} %get-tuple-element.333), channel_id=1, source_target_pairs={{4,0},{8,4},{12,8},{5,1},{9,5},{13,9},{6,2},{10,6},{14,10},{7,3},{... | collective-permute-start | bytes 15368 | tf_op jit(solution)/shard_map/ppermute | solution.py:18
  163.3 7.2 %collective-permute-start.22 = (f32[10,34,1]{2,1,0:T(8,128)S(1)}, f32[10,34,1]{2,1,0:T(8,128)S(1)}, u32[]{:S(2)}, u32[]{:S(2)}) collective-permute-start(f32[10,34,1]{2,1,0:T(8,128)S(1)} %get-tuple-element.330), channel_id=1, source_target_pairs={{0,1},{1,2},{2,3},{4,5},{5,6},{6,7},{8,9},{9,10},{10,11},{12,13},{... | collective-permute-start | bytes 4088 | tf_op jit(solution)/shard_map/ppermute | solution.py:15
  165.8 9.5 %collective-permute-start.23 = (f32[10,34,1]{2,1,0:T(8,128)S(1)}, f32[10,34,1]{2,1,0:T(8,128)S(1)}, u32[]{:S(2)}, u32[]{:S(2)}) collective-permute-start(f32[10,34,1]{2,1,0:T(8,128)S(1)} %get-tuple-element.331), channel_id=1, source_target_pairs={{1,0},{2,1},{3,2},{5,4},{6,5},{7,6},{9,8},{10,9},{11,10},{13,12},{... | collective-permute-start | bytes 4088 | tf_op jit(solution)/shard_map/ppermute | solution.py:18
  176.1 1.0 copy-start.2
  180.2 38.6 %copy-start.8 = (f32[9]{0:T(128)S(1)}, f32[9]{0:T(128)}, u32[]{:S(2)}) copy-start(f32[9]{0:T(128)} %constant.686.clone.1) | copy-start | bytes 112
  180.2 39.3 %copy-start.7 = (f32[9]{0:T(128)S(1)}, f32[9]{0:T(128)}, u32[]{:S(2)}) copy-start(f32[9]{0:T(128)} %constant.661.clone.1) | copy-start | bytes 112
  180.2 39.3 %copy-start.9 = (f32[9,1]{0,1:T(1,128)S(1)}, f32[9,1]{0,1:T(1,128)}, u32[]{:S(2)}) copy-start(f32[9,1]{0,1:T(1,128)} %constant.803) | copy-start | bytes 112
  238.7 12.8 %copy-start.3 = (f32[8,32,128]{2,1,0:T(8,128)S(1)}, f32[8,32,128]{2,1,0:T(8,128)}, u32[]{:S(2)}) copy-start(f32[8,32,128]{2,1,0:T(8,128)} %param.52) | copy-start | bytes 393220
